TPU v7x, 32 devices: a whole 2x2x4 slice. The times are simulated.
32 devices in a mesh: res: 8 (over z, y), ch: 4 (over x, core).
Axes of the slice: x: 2, y: 2, z: 4, core: 2. Of those that a mesh axis runs over, the one named last changes fastest.
Arguments:
- sequence_matrix: bfloat16 [8, 512, 256], P(None, 'res'), may hold values from -6 to 6
- couple_matrix: bfloat16 [32, 128, 4096], P('res', 'ch')
- block_target_entry: int32 [8, 4], P('res'), may hold values from 0 to 7, as said below
- block_present_flag: int32 [8, 4], P('res'), may hold values from 0 to 1, as said below
- amino_strand: int32 [512], P('res'), may hold values from 0 to 5, never falling along the last dimension, each value on 1 to 170 neighbouring positions
- sequence_scaling_factor: float32 [256], replicated, may hold values from 0.5 to 1.5
- query_key_value_matrix: bfloat16 [4, 256, 256], P(None, None, 'ch'), may hold values from -0.375 to 0.375
- focus_result_matrix: bfloat16 [256, 256], P('ch'), may hold values from -0.375 to 0.375
- strand_focus_offset: float32 [8], replicated, may hold values from -2 to 2
- couple_scaling_factor: float32 [128], P('ch'), may hold values from 0.5 to 1.5
- focus_offset_matrix: float32 [128, 8], P('ch')
- product_scaling_factor: float32 [256], replicated, may hold values from 0.5 to 1.5
- first_factor_matrix: bfloat16 [256, 32], replicated, may hold values from -0.375 to 0.375
- second_factor_matrix: bfloat16 [256, 32], P(None, 'ch'), may hold values from -0.375 to 0.375
- product_result_matrix: bfloat16 [128, 32, 32], P(None, None, 'ch'), may hold values from -0.8984375 to 0.8984375
- product_result_offset: float32 [128], P('ch'), may hold values from -3 to 3
Outputs:
- sequence_result_matrix: bfloat16 [8, 512, 256], P(None, 'res')
- pairwise_output: bfloat16 [32, 128, 4096], P('res', 'ch')
Inputs may be any that keep to these rules, and one draw needn't show every extreme that they name: `block_target_entry`: slot 0 of row tile r names r itself; the column tiles of one row tile are distinct. `block_present_flag`: the valid slots of each row tile are its first ones, two or more of them; in every draw some row tile has all 4 slots valid.
All inputs are finite; a program needn't handle non-finite values.
Results may differ from a plain program's by a relative error of at most 0.005.
Values may be sent and summed in bfloat16 or wider, within the bound.
No kernel may reach another device: no remote copies, remote signals or barrier semaphores. Data moves between devices by JAX's collectives and lax.ppermute only.
A program may use at most 128 MiB of HBM per device.

v0:
```python
import math
import jax
import jax.numpy as jnp
from jax import lax
from jax.sharding import PartitionSpec as P

C_Z = 128
FOCUS_NUMBER = 8
FOCUS_BREADTH = 32
PRODUCT_FEATURE = 32
EPS = 1e-05
MASKED = -1e30


def final_dimension_standardize(values, gain_vector):
    values = values.astype(jnp.float32)
    average = jnp.mean(values, axis=-1, keepdims=True)
    variance = jnp.mean(jnp.square(values - average), axis=-1, keepdims=True)
    return (values - average) * lax.rsqrt(variance + EPS) * gain_vector


def on_device(
    sequence_matrix,
    couple_matrix,
    block_target_entry,
    block_present_flag,
    amino_strand,
    sequence_scaling_factor,
    query_key_value_matrix,
    focus_result_matrix,
    strand_focus_offset,
    couple_scaling_factor,
    focus_offset_matrix,
    product_scaling_factor,
    first_factor_matrix,
    second_factor_matrix,
    product_result_matrix,
    product_result_offset,
):
    groups = lax.axis_size("ch")
    group_index = lax.axis_index("ch")
    local_heads = FOCUS_NUMBER // groups
    slot_count = couple_matrix.shape[0]
    cell_count = couple_matrix.shape[2]
    block_extent = sequence_matrix.shape[1]
    sequence_number_overall = sequence_matrix.shape[0]
    pair_field = couple_matrix.astype(jnp.float32)
    part_one = jnp.sum(pair_field, axis=1)
    part_two = jnp.sum(pair_field * pair_field, axis=1)
    sum_one, sum_two = lax.psum((part_one, part_two), "ch")
    center = sum_one / C_Z
    spread = lax.rsqrt(sum_two / C_Z - center * center + EPS)
    normed = (
        (pair_field - center[:, None, :])
        * spread[:, None, :]
        * couple_scaling_factor[None, :, None]
    )
    partial_value = jnp.einsum(
        "kcp,ch->hkp", normed, focus_offset_matrix, precision=lax.Precision.HIGHEST
    )
    head_bias = lax.psum_scatter(partial_value, "ch", scatter_dimension=0, tiled=True)
    head_bias = head_bias.astype(jnp.bfloat16)
    bias_all, cols_all, valid_all, chain_all = (
        lax.all_gather(head_bias, "res", axis=1, tiled=True),
        lax.all_gather(block_target_entry, "res", axis=0, tiled=True),
        lax.all_gather(block_present_flag, "res", axis=0, tiled=True),
        lax.all_gather(amino_strand, "res", axis=0, tiled=True),
    )
    sequence_first_layout = lax.all_to_all(
        sequence_matrix, "res", split_axis=0, concat_axis=1, tiled=True
    )
    device_rows, amino_number_here, sequence_feature_breadth = sequence_first_layout.shape
    tile_count = amino_number_here // block_extent
    sequence_standardized = final_dimension_standardize(
        sequence_first_layout, sequence_scaling_factor
    ).astype(jnp.bfloat16)
    projected_rows = jnp.einsum(
        "hbx,sxt->shbt",
        sequence_standardized,
        query_key_value_matrix,
        preferred_element_type=jnp.float32,
    ).astype(jnp.bfloat16)
    projected_rows = projected_rows.reshape(
        4, device_rows, tile_count, block_extent, local_heads, FOCUS_BREADTH
    )
    queries = projected_rows[0]
    keyset = projected_rows[1]
    valueset = projected_rows[2]
    gateset = projected_rows[3]
    chain_tiles = chain_all.reshape(tile_count, block_extent)
    bias_tiles = bias_all.reshape(local_heads, tile_count, slot_count, block_extent, block_extent)
    head_scale = lax.dynamic_slice_in_dim(
        strand_focus_offset, group_index * local_heads, local_heads, 0
    )
    block_tiles = math.gcd(tile_count, max(1, 512 // block_extent))

    def attend(block_index):
        first_tile = block_index * block_tiles
        columns = lax.dynamic_slice_in_dim(cols_all, first_tile, block_tiles, 0)
        usable = lax.dynamic_slice_in_dim(valid_all, first_tile, block_tiles, 0) > 0
        query_block = lax.dynamic_slice_in_dim(queries, first_tile, block_tiles, 1)
        key_block = keyset[:, columns]
        value_block = valueset[:, columns]
        scores = jnp.einsum(
            "rgahd,rgkbhd->rghakb", query_block, key_block, preferred_element_type=jnp.float32
        ) * FOCUS_BREADTH ** (-0.5)
        pair_part = lax.dynamic_slice_in_dim(bias_tiles, first_tile, block_tiles, 1).astype(
            jnp.float32
        )
        pair_part = pair_part.transpose(1, 0, 3, 2, 4)
        query_chain = lax.dynamic_slice_in_dim(chain_tiles, first_tile, block_tiles, 0)
        same_chain = (query_chain[:, :, None, None] == chain_tiles[columns][:, None, :, :]).astype(
            jnp.float32
        )
        scores = (
            scores
            + pair_part[None]
            + head_scale[None, None, :, None, None, None] * same_chain[None, :, None]
        )
        scores = jnp.where(usable[None, :, None, None, :, None], scores, MASKED)
        row_max = jnp.max(scores, axis=(4, 5), keepdims=True)
        exponent = jnp.exp(scores - row_max)
        attn_weights = (exponent / jnp.sum(exponent, axis=(4, 5), keepdims=True)).astype(
            jnp.bfloat16
        )
        mixed = jnp.einsum(
            "rghakb,rgkbhd->rgahd", attn_weights, value_block, preferred_element_type=jnp.float32
        )
        gate_block = lax.dynamic_slice_in_dim(gateset, first_tile, block_tiles, 1).astype(
            jnp.float32
        )
        return (mixed * jax.nn.sigmoid(gate_block)).astype(jnp.bfloat16)

    blocks = lax.map(attend, jnp.arange(tile_count // block_tiles, dtype=jnp.int32))
    attended_rows = blocks.transpose(1, 0, 2, 3, 4, 5).reshape(
        device_rows * amino_number_here, local_heads * FOCUS_BREADTH
    )
    residual_input = sequence_first_layout.reshape(
        device_rows * amino_number_here, sequence_feature_breadth
    )
    partial_out = jnp.dot(attended_rows, focus_result_matrix, preferred_element_type=jnp.float32)
    head_total = lax.psum(partial_out, "ch")
    updated_state = (
        (residual_input.astype(jnp.float32) + head_total)
        .astype(jnp.bfloat16)
        .reshape(device_rows, amino_number_here, sequence_feature_breadth)
    )
    sequence_result_matrix = lax.all_to_all(
        updated_state, "res", split_axis=1, concat_axis=0, tiled=True
    )
    outer_normed = (
        final_dimension_standardize(sequence_result_matrix, product_scaling_factor)
        .astype(jnp.bfloat16)
        .reshape(sequence_number_overall * block_extent, sequence_feature_breadth)
    )
    left_projected = (
        jnp.dot(outer_normed, first_factor_matrix, preferred_element_type=jnp.float32)
        .astype(jnp.bfloat16)
        .reshape(sequence_number_overall, block_extent * PRODUCT_FEATURE)
    )
    own_columns = block_target_entry[0]
    right_projected = (
        jnp.dot(outer_normed, second_factor_matrix, preferred_element_type=jnp.float32)
        .astype(jnp.bfloat16)
        .reshape(sequence_number_overall, block_extent, -1)
    )
    narrow = right_projected.shape[2]
    weight_flat = product_result_matrix.reshape(C_Z, PRODUCT_FEATURE * narrow)
    empty_tiles = jnp.zeros(
        (slot_count, sequence_number_overall, block_extent, narrow), jnp.bfloat16
    )
    shard_piece = lax.all_gather(right_projected, "res", axis=1, tiled=True)
    piece_rows = shard_piece.shape[1]
    offset = own_columns * block_extent
    inside = (offset >= 0) & (offset < piece_rows)

    def take_one(offset_one, inside_one, held_tile):
        taken = lax.dynamic_slice_in_dim(
            shard_piece, jnp.clip(offset_one, 0, piece_rows - block_extent), block_extent, 1
        )
        return jnp.where(inside_one, taken, held_tile)

    chosen = jax.vmap(take_one, in_axes=(0, 0, 0))(offset, inside, empty_tiles)
    left_turned = left_projected.T

    def outer_one(right_tile_rows):
        product = (
            jnp.dot(
                left_turned,
                right_tile_rows.reshape(sequence_number_overall, block_extent * narrow),
                preferred_element_type=jnp.float32,
            )
            / sequence_number_overall
        )
        product = (
            product.reshape(block_extent, PRODUCT_FEATURE, block_extent, narrow)
            .transpose(1, 3, 0, 2)
            .astype(jnp.bfloat16)
            .reshape(PRODUCT_FEATURE * narrow, cell_count)
        )
        return jnp.dot(weight_flat, product, preferred_element_type=jnp.float32)

    partials = lax.map(outer_one, chosen)
    summed = lax.psum_scatter(partials, "ch", scatter_dimension=1, tiled=True)
    keep_mask = block_present_flag[0].astype(jnp.float32)
    pairwise_output = (
        pair_field + keep_mask[:, None, None] * (summed + product_result_offset[None, :, None])
    ).astype(jnp.bfloat16)
    return (sequence_result_matrix, pairwise_output)


def solution(mesh):
    return jax.shard_map(
        on_device,
        mesh=mesh,
        in_specs=(
            P(None, "res", None),
            P("res", "ch", None),
            P("res", None),
            P("res", None),
            P("res"),
            P(),
            P(None, None, "ch"),
            P("ch", None),
            P(),
            P("ch"),
            P("ch", None),
            P(),
            P(),
            P(None, "ch"),
            P(None, None, "ch"),
            P("ch"),
        ),
        out_specs=(P(None, "res", None), P("res", "ch", None)),
        check_vma=False,
    )
```

profile of v0, /device:TPU:0, one launch (start us, length us, event | category | flops | bytes accessed | tf_op | source)
XLA Modules:
  0.0 450.4 jit_solution(9530738559762649015)
XLA Ops:
  7.2 7.5 %all-to-all-start = ((bf16[8,64,256]{2,1,0:T(8,128)(2,1)}), bf16[8,64,256]{2,1,0:T(8,128)(2,1)S(1)}, u32[]{:S(2)}, u32[]{:S(2)}) async-start(bf16[8,64,256]{2,1,0:T(8,128)(2,1)} %param.18), calls=%async_computation | async-start | bytes 524288 | tf_op jit(solution)/shard_map/all_to_all | solution.py:69
  20.0 11.8 %all-reduce = s32[512]{0:T(512)S(1)} all-reduce(s32[512]{0:T(512)S(1)} %dynamic-update-slice), channel_id=1, replica_groups=mesh['res'=8,'ch'=4] {'res'}, use_global_device_ids=true, to_apply=%add | all-reduce | flops 512 | bytes 4096
  31.9 17.9 %all-gather = s32[8,1,4]{2,1,0:T(1,128)S(1)} all-gather(s32[1,1,4]{2,1,0:T(1,128)} %bitcast.164), channel_id=1, replica_groups=mesh['res'=8,'ch'=4] {'res'}, dimensions={0}, use_global_device_ids=true | all-gather | bytes 144 | tf_op jit(solution)/shard_map/all_gather | solution.py:65
  51.9 16.8 %all-gather.1 = s32[8,1,4]{2,1,0:T(1,128)S(1)} all-gather(s32[1,1,4]{2,1,0:T(1,128)S(1)} %bitcast.165), channel_id=1, replica_groups=mesh['res'=8,'ch'=4] {'res'}, dimensions={0}, use_global_device_ids=true | all-gather | bytes 144 | tf_op jit(solution)/shard_map/all_gather | solution.py:66
  73.0 16.4 %all-reduce.10 = bf16[8,4,4096]{2,1,0:T(4,128)(2,1)S(1)} all-reduce(f32[8,4,4096]{2,1,0:T(4,128)S(1)} %copy.104), channel_id=2, replica_groups=mesh['res'=8,'ch'=4] {'ch'}, use_global_device_ids=true, to_apply=%region_6.0.clone | all-reduce | flops 131072 | bytes 786432
  89.5 31.4 %all_gather.17 = bf16[2,32,4096]{2,0,1:T(2,128)(2,1)S(1)} all-gather(bf16[2,4,4096]{2,0,1:T(2,128)(2,1)S(1)} %copy.105), channel_id=1, replica_groups=mesh['res'=8,'ch'=4] {'res'}, dimensions={1}, use_global_device_ids=true | all-gather | bytes 589824 | tf_op jit(solution)/shard_map/all_gather | solution.py:64
  136.4 31.8 %all-reduce.7.cloned.1.call-done = f32[512,256]{1,0:T(8,128)} async-done(((f32[512,256]{1,0:T(8,128)}), f32[512,256]{1,0:T(8,128)}) %all-reduce.7.cloned.1.call-update) | async-done | bytes 524304 | tf_op jit(solution)/shard_map/psum | solution.py:142
  179.1 8.0 %all-to-all-done.1 = bf16[8,2,8192]{2,1,0:T(2,128)(2,1)S(1)} async-done(((bf16[8,2,8192]{2,1,0:T(2,128)(2,1)}), bf16[8,2,8192]{2,1,0:T(2,128)(2,1)S(1)}, u32[]{:S(2)}, u32[]{:S(2)}) %all-to-all-start.1) | async-done | bytes 262176 | tf_op jit(solution)/shard_map/all_to_all | solution.py:148
  189.2 7.4 %multiply_reduce_fusion = f32[512]{0:T(512)S(1)} fusion(f32[512]{0:T(512)S(1)} %broadcast_multiply_fusion.2, bf16[512,1,256]{2,1,0:T(2,128)(2,1)S(1)} %reshape.379), kind=kLoop, calls=%fused_computation.49 | loop fusion | flops 523776 | bytes 266240 | tf_op jit(solution)/shard_map/reduce_sum | solution.py:18
  197.2 33.1 %all_gather.19 = bf16[8,512,8]{2,0,1:T(8,128)(2,1)S(1)} all-gather(bf16[8,64,8]{2,0,1:T(8,128)(2,1)S(1)} %copy.113), channel_id=1, replica_groups=mesh['res'=8,'ch'=4] {'res'}, dimensions={1}, use_global_device_ids=true | all-gather | bytes 73728 | tf_op jit(solution)/shard_map/all_gather | solution.py:172
  231.6 139.8 %while.2 = (s32[]{:T(128)}, f32[4,128,4096]{2,1,0:T(8,128)}, bf16[4,8,64,8]{3,1,2,0:T(8,128)(2,1)S(1)}, bf16[2048,8]{0,1:T(8,128)(2,1)S(1)}, bf16[128,256]{1,0:T(8,128)(2,1)S(1)}, /*index=5*/s32[]{:T(128)}) while((s32[]{:T(128)}, f32[4,128,4096]{2,1,0:T(8,128)}, bf16[4,8,64,8]{3,1,2,0:T(8,128)(2,1)S(1)}, bf16[2048,8]{0,1:T(8,128)(2,1)S(1)}, ...), condition=%wide.region_13.14_spmd, body=%wide.region_12.13_spmd.sunk | while | flops 287309824 | bytes 27418708 | solution.py:203
  232.6 8.1 %convert_element_type.203 = bf16[64,32,64,8]{1,0,3,2:T(8,128)(2,1)} reshape(bf16[2048,512]{0,1:T(8,128)(2,1)S(1)} %fusion.55) | data formatting | bytes 4194304 | tf_op jit(solution)/shard_map/while/body/eval_jaxpr/convert_element_type | solution.py:198
  240.7 14.6 %copy.154 = bf16[32,8,64,64]{3,2,1,0:T(8,128)(2,1)} copy(bf16[32,8,64,64]{0,2,1,3:T(8,128)(2,1)} %bitcast.151) | data formatting | bytes 4194304 | tf_op jit(solution)/shard_map/while/body/eval_jaxpr/convert_element_type | solution.py:198
  255.3 5.7 %reshape.383 = bf16[256,4096]{1,0:T(8,128)(2,1)S(1)} reshape(bf16[32,8,64,64]{3,2,1,0:T(8,128)(2,1)} %copy.154) | data formatting | bytes 4194304 | tf_op jit(solution)/shard_map/while/body/eval_jaxpr/reshape | solution.py:199
  267.6 8.1 %convert_element_type.203 = bf16[64,32,64,8]{1,0,3,2:T(8,128)(2,1)} reshape(bf16[2048,512]{0,1:T(8,128)(2,1)S(1)} %fusion.55) | data formatting | bytes 4194304 | tf_op jit(solution)/shard_map/while/body/eval_jaxpr/convert_element_type | solution.py:198
  275.7 14.6 %copy.154 = bf16[32,8,64,64]{3,2,1,0:T(8,128)(2,1)} copy(bf16[32,8,64,64]{0,2,1,3:T(8,128)(2,1)} %bitcast.151) | data formatting | bytes 4194304 | tf_op jit(solution)/shard_map/while/body/eval_jaxpr/convert_element_type | solution.py:198
  290.3 5.7 %reshape.383 = bf16[256,4096]{1,0:T(8,128)(2,1)S(1)} reshape(bf16[32,8,64,64]{3,2,1,0:T(8,128)(2,1)} %copy.154) | data formatting | bytes 4194304 | tf_op jit(solution)/shard_map/while/body/eval_jaxpr/reshape | solution.py:199
  302.5 8.1 %convert_element_type.203 = bf16[64,32,64,8]{1,0,3,2:T(8,128)(2,1)} reshape(bf16[2048,512]{0,1:T(8,128)(2,1)S(1)} %fusion.55) | data formatting | bytes 4194304 | tf_op jit(solution)/shard_map/while/body/eval_jaxpr/convert_element_type | solution.py:198
  310.6 14.6 %copy.154 = bf16[32,8,64,64]{3,2,1,0:T(8,128)(2,1)} copy(bf16[32,8,64,64]{0,2,1,3:T(8,128)(2,1)} %bitcast.151) | data formatting | bytes 4194304 | tf_op jit(solution)/shard_map/while/body/eval_jaxpr/convert_element_type | solution.py:198
  325.2 5.7 %reshape.383 = bf16[256,4096]{1,0:T(8,128)(2,1)S(1)} reshape(bf16[32,8,64,64]{3,2,1,0:T(8,128)(2,1)} %copy.154) | data formatting | bytes 4194304 | tf_op jit(solution)/shard_map/while/body/eval_jaxpr/reshape | solution.py:199
  337.4 8.1 %convert_element_type.203 = bf16[64,32,64,8]{1,0,3,2:T(8,128)(2,1)} reshape(bf16[2048,512]{0,1:T(8,128)(2,1)S(1)} %fusion.55) | data formatting | bytes 4194304 | tf_op jit(solution)/shard_map/while/body/eval_jaxpr/convert_element_type | solution.py:198
  345.6 14.6 %copy.154 = bf16[32,8,64,64]{3,2,1,0:T(8,128)(2,1)} copy(bf16[32,8,64,64]{0,2,1,3:T(8,128)(2,1)} %bitcast.151) | data formatting | bytes 4194304 | tf_op jit(solution)/shard_map/while/body/eval_jaxpr/convert_element_type | solution.py:198
  360.2 5.7 %reshape.383 = bf16[256,4096]{1,0:T(8,128)(2,1)S(1)} reshape(bf16[32,8,64,64]{3,2,1,0:T(8,128)(2,1)} %copy.154) | data formatting | bytes 4194304 | tf_op jit(solution)/shard_map/while/body/eval_jaxpr/reshape | solution.py:199
  372.2 68.8 %reduce-scatter.2.cloned.1.call-done = f32[4,32,4096]{2,1,0:T(8,128)} async-done(((f32[4,128,4096]{2,1,0:T(8,128)}), f32[4,32,4096]{2,1,0:T(8,128)}) %reduce-scatter.2.cloned.1.call-update) | async-done | bytes 2097168 | tf_op jit(solution)/shard_map/reduce_scatter | solution.py:204
  (149 shorter events, 70.5 us)
Async XLA Ops:
  7.2 119.0 %copy-start = (bf16[4,256,64]{1,2,0:T(8,128)(2,1)S(1)}, bf16[4,256,64]{1,2,0:T(8,128)(2,1)}, u32[]{:S(2)}) copy-start(bf16[4,256,64]{1,2,0:T(8,128)(2,1)} %param.24) | copy-start | bytes 393220
  7.2 61.8 %copy-start.17 = (u32[32]{0:T(128)S(1)}, u32[32]{0:T(128)}, u32[]{:S(2)}) copy-start(u32[32]{0:T(128)} %constant.112) | copy-start | bytes 388
  7.2 64.0 %copy-start.1 = (bf16[4,32,4096]{2,1,0:T(8,128)(2,1)S(1)}, bf16[4,32,4096]{2,1,0:T(8,128)(2,1)}, u32[]{:S(2)}) copy-start(bf16[4,32,4096]{2,1,0:T(8,128)(2,1)} %param.19) | copy-start | bytes 3145732
  7.2 44.7 %copy-start.13 = (s32[1,4]{1,0:T(1,128)S(1)}, s32[1,4]{1,0:T(1,128)}, u32[]{:S(2)}) copy-start(s32[1,4]{1,0:T(1,128)} %param.21) | copy-start | bytes 52
  7.2 61.7 %copy-start.15 = (f32[8]{0:T(128)S(1)}, f32[8]{0:T(128)}, u32[]{:S(2)}) copy-start(f32[8]{0:T(128)} %param.26) | copy-start | bytes 100
  7.2 64.0 %copy-start.16 = (f32[32]{0:T(128)S(1)}, f32[32]{0:T(128)}, u32[]{:S(2)}) copy-start(f32[32]{0:T(128)} %param.27) | copy-start | bytes 388
  7.2 64.0 %copy-start.14 = (f32[32,8]{0,1:T(8,128)S(1)}, f32[32,8]{0,1:T(8,128)}, u32[]{:S(2)}) copy-start(f32[32,8]{0,1:T(8,128)} %param.28) | copy-start | bytes 3076
  7.2 118.2 %all-to-all-start = ((bf16[8,64,256]{2,1,0:T(8,128)(2,1)}), bf16[8,64,256]{2,1,0:T(8,128)(2,1)S(1)}, u32[]{:S(2)}, u32[]{:S(2)}) async-start(bf16[8,64,256]{2,1,0:T(8,128)(2,1)} %param.18), calls=%async_computation | async-start | bytes 524288 | tf_op jit(solution)/shard_map/all_to_all | solution.py:69
  14.7 55.5 %all-reduce.9.cloned.1.call-start = ((), (), s32[]{:S(2)}) async-start(), calls=%async_computation.5 | async-start | bytes 262144 | tf_op jit(solution)/shard_map/psum | solution.py:50
  17.1 151.0 %all-reduce.7.cloned.1.call-start = ((), (), s32[]{:S(2)}) async-start(), calls=%async_computation.3 | async-start | bytes 1048576 | tf_op jit(solution)/shard_map/psum | solution.py:142
  123.5 2.5 copy-start.9
  133.4 1.0 copy-start.3
  133.4 1.1 copy-start.4
  134.5 0.8 copy-start.6
  136.3 42.6 %copy-start.5 = (bf16[128,32,8]{0,2,1:T(8,128)(2,1)S(1)}, bf16[128,32,8]{0,2,1:T(8,128)(2,1)}, u32[]{:S(2)}) copy-start(bf16[128,32,8]{0,2,1:T(8,128)(2,1)} %param.32) | copy-start | bytes 196612
  136.3 42.7 %copy-start.12 = (s32[1,4]{1,0:T(1,128)S(1)}, s32[1,4]{1,0:T(1,128)}, u32[]{:S(2)}) copy-start(s32[1,4]{1,0:T(1,128)} %param.20) | copy-start | bytes 52
  172.4 24.2 %copy-start.10 = (f32[256]{0:T(256)S(1)}, f32[256]{0:T(256)}, u32[]{:S(2)}) copy-start(f32[256]{0:T(256)} %param.29) | copy-start | bytes 3076
  173.2 23.6 %copy-start.8 = (bf16[256,8]{0,1:T(8,128)(2,1)S(1)}, bf16[256,8]{0,1:T(8,128)(2,1)}, u32[]{:S(2)}) copy-start(bf16[256,8]{0,1:T(8,128)(2,1)} %param.31) | copy-start | bytes 12292
  173.2 13.9 %all-to-all-start.1 = ((bf16[8,2,8192]{2,1,0:T(2,128)(2,1)}), bf16[8,2,8192]{2,1,0:T(2,128)(2,1)S(1)}, u32[]{:S(2)}, u32[]{:S(2)}) async-start(bf16[8,2,8192]{2,1,0:T(2,128)(2,1)} %reshape.378), calls=%async_computation.1 | async-start | bytes 524288 | tf_op jit(solution)/shard_map/all_to_all | solution.py:148
  178.8 262.1 %reduce-scatter.2.cloned.1.call-start = ((), (), s32[]{:S(2)}) async-start(), calls=%async_computation.4 | async-start | bytes 10485760 | tf_op jit(solution)/shard_map/reduce_scatter | solution.py:204
  187.3 43.0 %copy-start.7 = (bf16[256,32]{0,1:T(8,128)(2,1)S(1)}, bf16[256,32]{0,1:T(8,128)(2,1)}, u32[]{:S(2)}) copy-start(bf16[256,32]{0,1:T(8,128)(2,1)} %param.30) | copy-start | bytes 49156
  371.4 69.5 %copy-start.2 = (bf16[4,32,4096]{2,1,0:T(8,128)(2,1)S(1)}, bf16[4,32,4096]{2,1,0:T(8,128)(2,1)}, u32[]{:S(2)}) copy-start(bf16[4,32,4096]{2,1,0:T(8,128)(2,1)} %param.19) | copy-start | bytes 3145732
  371.4 69.5 %copy-start.11 = (f32[32]{0:T(128)S(1)}, f32[32]{0:T(128)}, u32[]{:S(2)}) copy-start(f32[32]{0:T(128)} %param.33) | copy-start | bytes 388
Sparse Core Ops, SparseCore 0:
  18.5 33.1 all-reduce.8
  136.5 31.6 all-reduce.6
  371.6 69.3 reduce-scatter.1
where the time goes:
time: 452 us; the launch traced here: 450 us
  local copies, waits for them, and re-layouts  146 us (32%)
  blocking collectives  127 us (28%)
  waiting for transfers between devices  109 us (24%)
  other arithmetic  21.8 us (5%)
  matrix products  17.3 us (4%)
  between operations  15.5 us (3%)
  starting transfers between devices  13.2 us (3%)
    convert_element_type x8, local copies, waits for them, and re-layouts, outer_one(): product = product.reshape(block_extent, PRODUCT_FEATURE, block_extent, na...  90.9 us
    reduce_scatter x1, waiting for transfers between devices, on_device(): summed = lax.psum_scatter(partials, 'ch', scatter_dimension=1, tiled=True)  68.8 us
    all_gather x1, blocking collectives, on_device(): shard_piece = lax.all_gather(right_projected, 'res', axis=1, tiled=True)  33.1 us
    psum x1, waiting for transfers between devices, on_device(): head_total = lax.psum(partial_out, 'ch')  31.8 us
    all_gather x1, blocking collectives, on_device(): lax.all_gather(head_bias, 'res', axis=1, tiled=True)  31.4 us
    unnamed x2, blocking collectives  28.2 us
    reshape x4, local copies, waits for them, and re-layouts, outer_one(): product = product.reshape(block_extent, PRODUCT_FEATURE, block_extent, na...  22.7 us
    all_gather x1, blocking collectives, on_device(): lax.all_gather(block_target_entry, 'res', axis=0, tiled=True)  17.9 us
  transfers between devices with their start and end apart: 5, of which 3 were waited for; matrix products, arithmetic and copies ran while one was open for 4% of the time, Pallas kernels for 0%

commit v1 on v0

--- a/solution.py
+++ b/solution.py
@@ -10,6 +10,12 @@
 PRODUCT_FEATURE = 32
 EPS = 1e-05
 MASKED = -1e30
+
+
+def in_order(blocks, dim):
+    blocks = jnp.moveaxis(blocks, 0, dim)
+    dims = blocks.shape
+    return blocks.reshape(*dims[:dim], dims[dim] * dims[dim + 1], *dims[dim + 2 :])
 
 
 def final_dimension_standardize(values, gain_vector):
@@ -169,7 +175,19 @@
     empty_tiles = jnp.zeros(
         (slot_count, sequence_number_overall, block_extent, narrow), jnp.bfloat16
     )
-    shard_piece = lax.all_gather(right_projected, "res", axis=1, tiled=True)
+    size = lax.axis_size("res")
+    pairs = [(i, (i + 1) % size) for i in range(size)]
+    back = [(b, a) for a, b in pairs]
+    lower, upper = ([], [])
+    for hop in range(size - 1):
+        if hop % 2 == 0:
+            lower.append(lax.ppermute(lower[-1] if lower else right_projected, "res", pairs))
+        else:
+            upper.append(lax.ppermute(upper[-1] if upper else right_projected, "res", back))
+    blocks_2 = jnp.stack([*lower[::-1], right_projected, *upper])
+    shift = lax.axis_index("res") - len(lower)
+    blocks_2 = blocks_2[(jnp.arange(size) - shift) % size]
+    shard_piece = in_order(blocks_2, 1)
     piece_rows = shard_piece.shape[1]
     offset = own_columns * block_extent
     inside = (offset >= 0) & (offset < piece_rows)

time: 452 us -> 448 us (level)
  blocking collectives: 127 us -> 94.3 us
  starting transfers between devices: 13.2 us -> 28.9 us
  waiting for transfers between devices: 109 us -> 122 us
    all_gather x1 -> x0, blocking collectives: 33.1 us -> none  [on_device(): shard_piece = lax.all_gather(right_projected, 'res', axis=1, tiled=True)]
    ppermute x0 -> x7, starting transfers between devices: none -> 15.7 us  [the longest x3 14.3 us: on_device(): lax.ppermute(upper[-1] if upper else right_projected, 'res', back)]
    ppermute x0 -> x7, waiting for transfers between devices: none -> 9.62 us  [the longest x4 9.3 us: on_device(): lax.ppermute(lower[-1] if lower else right_projected, 'res', pairs)]
  transfers between devices with their start and end apart: 5 -> 12, of which waited for: 3 -> 8; matrix products, arithmetic and copies ran while one was open for 4% -> 4% of each run, Pallas kernels for 0% -> 0%
where the time goes in v1:
time: 448 us; the launch traced here: 447 us
  local copies, waits for them, and re-layouts  148 us (33%)
  waiting for transfers between devices  122 us (27%)
  blocking collectives  94.3 us (21%)
  starting transfers between devices  28.9 us (6%)
  other arithmetic  21.8 us (5%)
  matrix products  17.2 us (4%)
  between operations  15.5 us (3%)
    convert_element_type x8, local copies, waits for them, and re-layouts, outer_one(): product = product.reshape(block_extent, PRODUCT_FEATURE, block_extent, na...  90.9 us
    reduce_scatter x1, waiting for transfers between devices, on_device(): summed = lax.psum_scatter(partials, 'ch', scatter_dimension=1, tiled=True)  71.9 us
    psum x1, waiting for transfers between devices, on_device(): head_total = lax.psum(partial_out, 'ch')  31.8 us
    all_gather x1, blocking collectives, on_device(): lax.all_gather(head_bias, 'res', axis=1, tiled=True)  31.4 us
    unnamed x2, blocking collectives  28.2 us
    reshape x4, local copies, waits for them, and re-layouts, outer_one(): product = product.reshape(block_extent, PRODUCT_FEATURE, block_extent, na...  22.7 us
    all_gather x1, blocking collectives, on_device(): lax.all_gather(block_target_entry, 'res', axis=0, tiled=True)  17.9 us
    all_gather x1, blocking collectives, on_device(): lax.all_gather(block_present_flag, 'res', axis=0, tiled=True)  16.8 us
  transfers between devices with their start and end apart: 12, of which 8 were waited for; matrix products, arithmetic and copies ran while one was open for 4% of the time, Pallas kernels for 0%

profile of v1, /device:TPU:0, one launch (start us, length us, event | category | flops | bytes accessed | tf_op | source)
XLA Modules:
  0.0 446.9 jit_solution(1716009650096445688)
XLA Ops:
  7.2 7.5 %all-to-all-start = ((bf16[8,64,256]{2,1,0:T(8,128)(2,1)}), bf16[8,64,256]{2,1,0:T(8,128)(2,1)S(1)}, u32[]{:S(2)}, u32[]{:S(2)}) async-start(bf16[8,64,256]{2,1,0:T(8,128)(2,1)} %param.18), calls=%async_computation | async-start | bytes 524288 | tf_op jit(solution)/shard_map/all_to_all | solution.py:75
  20.0 11.8 %all-reduce = s32[512]{0:T(512)S(1)} all-reduce(s32[512]{0:T(512)S(1)} %dynamic-update-slice), channel_id=1, replica_groups=mesh['res'=8,'ch'=4] {'res'}, use_global_device_ids=true, to_apply=%add | all-reduce | flops 512 | bytes 4096
  31.9 17.9 %all-gather = s32[8,1,4]{2,1,0:T(1,128)S(1)} all-gather(s32[1,1,4]{2,1,0:T(1,128)} %bitcast.186), channel_id=1, replica_groups=mesh['res'=8,'ch'=4] {'res'}, dimensions={0}, use_global_device_ids=true | all-gather | bytes 144 | tf_op jit(solution)/shard_map/all_gather | solution.py:71
  51.9 16.8 %all-gather.1 = s32[8,1,4]{2,1,0:T(1,128)S(1)} all-gather(s32[1,1,4]{2,1,0:T(1,128)S(1)} %bitcast.187), channel_id=1, replica_groups=mesh['res'=8,'ch'=4] {'res'}, dimensions={0}, use_global_device_ids=true | all-gather | bytes 144 | tf_op jit(solution)/shard_map/all_gather | solution.py:72
  73.0 16.4 %all-reduce.10 = bf16[8,4,4096]{2,1,0:T(4,128)(2,1)S(1)} all-reduce(f32[8,4,4096]{2,1,0:T(4,128)S(1)} %copy.104), channel_id=2, replica_groups=mesh['res'=8,'ch'=4] {'ch'}, use_global_device_ids=true, to_apply=%region_6.0.clone | all-reduce | flops 131072 | bytes 786432
  89.5 31.4 %all_gather.14 = bf16[2,32,4096]{2,0,1:T(2,128)(2,1)S(1)} all-gather(bf16[2,4,4096]{2,0,1:T(2,128)(2,1)S(1)} %copy.105), channel_id=1, replica_groups=mesh['res'=8,'ch'=4] {'res'}, dimensions={1}, use_global_device_ids=true | all-gather | bytes 589824 | tf_op jit(solution)/shard_map/all_gather | solution.py:70
  136.3 31.8 %all-reduce.7.cloned.1.call-done = f32[512,256]{1,0:T(8,128)} async-done(((f32[512,256]{1,0:T(8,128)}), f32[512,256]{1,0:T(8,128)}) %all-reduce.7.cloned.1.call-update) | async-done | bytes 524304 | tf_op jit(solution)/shard_map/psum | solution.py:148
  173.2 5.6 %all-to-all-start.1 = ((bf16[8,2,8192]{2,1,0:T(2,128)(2,1)}), bf16[8,2,8192]{2,1,0:T(2,128)(2,1)S(1)}, u32[]{:S(2)}, u32[]{:S(2)}) async-start(bf16[8,2,8192]{2,1,0:T(2,128)(2,1)} %reshape.439), calls=%async_computation.1 | async-start | bytes 524288 | tf_op jit(solution)/shard_map/all_to_all | solution.py:154
  178.9 8.1 %all-to-all-done.1 = bf16[8,2,8192]{2,1,0:T(2,128)(2,1)S(1)} async-done(((bf16[8,2,8192]{2,1,0:T(2,128)(2,1)}), bf16[8,2,8192]{2,1,0:T(2,128)(2,1)S(1)}, u32[]{:S(2)}, u32[]{:S(2)}) %all-to-all-start.1) | async-done | bytes 262176 | tf_op jit(solution)/shard_map/all_to_all | solution.py:154
  189.1 7.4 %multiply_reduce_fusion = f32[512]{0:T(512)S(1)} fusion(f32[512]{0:T(512)S(1)} %broadcast_multiply_fusion.2, bf16[512,1,256]{2,1,0:T(2,128)(2,1)S(1)} %reshape.440), kind=kLoop, calls=%fused_computation.50 | loop fusion | flops 523776 | bytes 266240 | tf_op jit(solution)/shard_map/reduce_sum | solution.py:24
  225.1 139.6 %while.2 = (s32[]{:T(128)}, f32[4,128,4096]{2,1,0:T(8,128)}, bf16[4,8,64,8]{3,1,2,0:T(8,128)(2,1)S(1)}, bf16[2048,8]{0,1:T(8,128)(2,1)S(1)}, bf16[128,256]{1,0:T(8,128)(2,1)S(1)}, /*index=5*/s32[]{:T(128)}) while((s32[]{:T(128)}, f32[4,128,4096]{2,1,0:T(8,128)}, bf16[4,8,64,8]{3,1,2,0:T(8,128)(2,1)S(1)}, bf16[2048,8]{0,1:T(8,128)(2,1)S(1)}, ...), condition=%wide.region_13.14_spmd, body=%wide.region_12.13_spmd.sunk | while | flops 287309824 | bytes 27418708 | solution.py:221
  226.1 8.1 %convert_element_type.203 = bf16[64,32,64,8]{1,0,3,2:T(8,128)(2,1)} reshape(bf16[2048,512]{0,1:T(8,128)(2,1)S(1)} %fusion.57) | data formatting | bytes 4194304 | tf_op jit(solution)/shard_map/while/body/eval_jaxpr/convert_element_type | solution.py:216
  234.2 14.6 %copy.154 = bf16[32,8,64,64]{3,2,1,0:T(8,128)(2,1)} copy(bf16[32,8,64,64]{0,2,1,3:T(8,128)(2,1)} %bitcast.171) | data formatting | bytes 4194304 | tf_op jit(solution)/shard_map/while/body/eval_jaxpr/convert_element_type | solution.py:216
  248.9 5.7 %reshape.444 = bf16[256,4096]{1,0:T(8,128)(2,1)S(1)} reshape(bf16[32,8,64,64]{3,2,1,0:T(8,128)(2,1)} %copy.154) | data formatting | bytes 4194304 | tf_op jit(solution)/shard_map/while/body/eval_jaxpr/reshape | solution.py:217
  261.0 8.1 %convert_element_type.203 = bf16[64,32,64,8]{1,0,3,2:T(8,128)(2,1)} reshape(bf16[2048,512]{0,1:T(8,128)(2,1)S(1)} %fusion.57) | data formatting | bytes 4194304 | tf_op jit(solution)/shard_map/while/body/eval_jaxpr/convert_element_type | solution.py:216
  269.1 14.6 %copy.154 = bf16[32,8,64,64]{3,2,1,0:T(8,128)(2,1)} copy(bf16[32,8,64,64]{0,2,1,3:T(8,128)(2,1)} %bitcast.171) | data formatting | bytes 4194304 | tf_op jit(solution)/shard_map/while/body/eval_jaxpr/convert_element_type | solution.py:216
  283.8 5.7 %reshape.444 = bf16[256,4096]{1,0:T(8,128)(2,1)S(1)} reshape(bf16[32,8,64,64]{3,2,1,0:T(8,128)(2,1)} %copy.154) | data formatting | bytes 4194304 | tf_op jit(solution)/shard_map/while/body/eval_jaxpr/reshape | solution.py:217
  295.9 8.1 %convert_element_type.203 = bf16[64,32,64,8]{1,0,3,2:T(8,128)(2,1)} reshape(bf16[2048,512]{0,1:T(8,128)(2,1)S(1)} %fusion.57) | data formatting | bytes 4194304 | tf_op jit(solution)/shard_map/while/body/eval_jaxpr/convert_element_type | solution.py:216
  304.0 14.6 %copy.154 = bf16[32,8,64,64]{3,2,1,0:T(8,128)(2,1)} copy(bf16[32,8,64,64]{0,2,1,3:T(8,128)(2,1)} %bitcast.171) | data formatting | bytes 4194304 | tf_op jit(solution)/shard_map/while/body/eval_jaxpr/convert_element_type | solution.py:216
  318.6 5.7 %reshape.444 = bf16[256,4096]{1,0:T(8,128)(2,1)S(1)} reshape(bf16[32,8,64,64]{3,2,1,0:T(8,128)(2,1)} %copy.154) | data formatting | bytes 4194304 | tf_op jit(solution)/shard_map/while/body/eval_jaxpr/reshape | solution.py:217
  330.8 8.1 %convert_element_type.203 = bf16[64,32,64,8]{1,0,3,2:T(8,128)(2,1)} reshape(bf16[2048,512]{0,1:T(8,128)(2,1)S(1)} %fusion.57) | data formatting | bytes 4194304 | tf_op jit(solution)/shard_map/while/body/eval_jaxpr/convert_element_type | solution.py:216
  338.9 14.6 %copy.154 = bf16[32,8,64,64]{3,2,1,0:T(8,128)(2,1)} copy(bf16[32,8,64,64]{0,2,1,3:T(8,128)(2,1)} %bitcast.171) | data formatting | bytes 4194304 | tf_op jit(solution)/shard_map/while/body/eval_jaxpr/convert_element_type | solution.py:216
  353.5 5.7 %reshape.444 = bf16[256,4096]{1,0:T(8,128)(2,1)S(1)} reshape(bf16[32,8,64,64]{3,2,1,0:T(8,128)(2,1)} %copy.154) | data formatting | bytes 4194304 | tf_op jit(solution)/shard_map/while/body/eval_jaxpr/reshape | solution.py:217
  365.5 71.9 %reduce-scatter.2.cloned.1.call-done = f32[4,32,4096]{2,1,0:T(8,128)} async-done(((f32[4,128,4096]{2,1,0:T(8,128)}), f32[4,32,4096]{2,1,0:T(8,128)}) %reduce-scatter.2.cloned.1.call-update) | async-done | bytes 2097168 | tf_op jit(solution)/shard_map/reduce_scatter | solution.py:222
  (174 shorter events, 91.1 us)
Async XLA Ops:
  7.2 119.0 %copy-start = (bf16[4,256,64]{1,2,0:T(8,128)(2,1)S(1)}, bf16[4,256,64]{1,2,0:T(8,128)(2,1)}, u32[]{:S(2)}) copy-start(bf16[4,256,64]{1,2,0:T(8,128)(2,1)} %param.24) | copy-start | bytes 393220
  7.2 61.8 %copy-start.17 = (u32[32]{0:T(128)S(1)}, u32[32]{0:T(128)}, u32[]{:S(2)}) copy-start(u32[32]{0:T(128)} %constant.134) | copy-start | bytes 388
  7.2 64.0 %copy-start.1 = (bf16[4,32,4096]{2,1,0:T(8,128)(2,1)S(1)}, bf16[4,32,4096]{2,1,0:T(8,128)(2,1)}, u32[]{:S(2)}) copy-start(bf16[4,32,4096]{2,1,0:T(8,128)(2,1)} %param.19) | copy-start | bytes 3145732
  7.2 44.7 %copy-start.13 = (s32[1,4]{1,0:T(1,128)S(1)}, s32[1,4]{1,0:T(1,128)}, u32[]{:S(2)}) copy-start(s32[1,4]{1,0:T(1,128)} %param.21) | copy-start | bytes 52
  7.2 61.7 %copy-start.15 = (f32[8]{0:T(128)S(1)}, f32[8]{0:T(128)}, u32[]{:S(2)}) copy-start(f32[8]{0:T(128)} %param.26) | copy-start | bytes 100
  7.2 64.0 %copy-start.16 = (f32[32]{0:T(128)S(1)}, f32[32]{0:T(128)}, u32[]{:S(2)}) copy-start(f32[32]{0:T(128)} %param.27) | copy-start | bytes 388
  7.2 64.0 %copy-start.14 = (f32[32,8]{0,1:T(8,128)S(1)}, f32[32,8]{0,1:T(8,128)}, u32[]{:S(2)}) copy-start(f32[32,8]{0,1:T(8,128)} %param.28) | copy-start | bytes 3076
  7.2 118.1 %all-to-all-start = ((bf16[8,64,256]{2,1,0:T(8,128)(2,1)}), bf16[8,64,256]{2,1,0:T(8,128)(2,1)S(1)}, u32[]{:S(2)}, u32[]{:S(2)}) async-start(bf16[8,64,256]{2,1,0:T(8,128)(2,1)} %param.18), calls=%async_computation | async-start | bytes 524288 | tf_op jit(solution)/shard_map/all_to_all | solution.py:75
  14.7 55.5 %all-reduce.9.cloned.1.call-start = ((), (), s32[]{:S(2)}) async-start(), calls=%async_computation.5 | async-start | bytes 262144 | tf_op jit(solution)/shard_map/psum | solution.py:56
  17.1 151.0 %all-reduce.7.cloned.1.call-start = ((), (), s32[]{:S(2)}) async-start(), calls=%async_computation.3 | async-start | bytes 1048576 | tf_op jit(solution)/shard_map/psum | solution.py:148
  136.3 42.6 %copy-start.12 = (s32[1,4]{1,0:T(1,128)S(1)}, s32[1,4]{1,0:T(1,128)}, u32[]{:S(2)}) copy-start(s32[1,4]{1,0:T(1,128)} %param.20) | copy-start | bytes 52
  173.2 13.9 %all-to-all-start.1 = ((bf16[8,2,8192]{2,1,0:T(2,128)(2,1)}), bf16[8,2,8192]{2,1,0:T(2,128)(2,1)S(1)}, u32[]{:S(2)}, u32[]{:S(2)}) async-start(bf16[8,2,8192]{2,1,0:T(2,128)(2,1)} %reshape.439), calls=%async_computation.1 | async-start | bytes 524288 | tf_op jit(solution)/shard_map/all_to_all | solution.py:154
  178.8 31.1 %copy-start.5 = (bf16[128,32,8]{0,2,1:T(8,128)(2,1)S(1)}, bf16[128,32,8]{0,2,1:T(8,128)(2,1)}, u32[]{:S(2)}) copy-start(bf16[128,32,8]{0,2,1:T(8,128)(2,1)} %param.32) | copy-start | bytes 196612
  178.8 37.5 %copy-start.7 = (bf16[256,32]{0,1:T(8,128)(2,1)S(1)}, bf16[256,32]{0,1:T(8,128)(2,1)}, u32[]{:S(2)}) copy-start(bf16[256,32]{0,1:T(8,128)(2,1)} %param.30) | copy-start | bytes 49156
  178.8 258.6 %reduce-scatter.2.cloned.1.call-start = ((), (), s32[]{:S(2)}) async-start(), calls=%async_computation.4 | async-start | bytes 10485760 | tf_op jit(solution)/shard_map/reduce_scatter | solution.py:222
  197.0 6.4 %collective-permute-start = (bf16[8,64,8]{1,0,2:T(8,128)(2,1)S(1)}, bf16[8,64,8]{1,0,2:T(8,128)(2,1)S(1)}, u32[]{:S(2)}, u32[]{:S(2)}) collective-permute-start(bf16[8,64,8]{1,0,2:T(8,128)(2,1)S(1)} %reshape.358), channel_id=1, source_target_pairs={{0,4},{4,8},{8,12},{12,16},{16,20},{20,24},{24,28},{28,0},{1,5},{5... | collective-permute-start | bytes 24584 | tf_op jit(solution)/shard_map/ppermute | solution.py:184
  203.5 6.4 %collective-permute-start.1 = (bf16[8,64,8]{1,0,2:T(8,128)(2,1)S(1)}, bf16[8,64,8]{1,0,2:T(8,128)(2,1)S(1)}, u32[]{:S(2)}, u32[]{:S(2)}) collective-permute-start(bf16[8,64,8]{1,0,2:T(8,128)(2,1)S(1)} %collective-permute-done), channel_id=1, source_target_pairs={{0,4},{4,8},{8,12},{12,16},{16,20},{20,24},{24,28},{28,0},{1,5},{5... | collective-permute-start | bytes 24584 | tf_op jit(solution)/shard_map/ppermute | solution.py:184
  203.5 6.6 %collective-permute-start.4 = (bf16[8,64,8]{1,0,2:T(8,128)(2,1)S(1)}, bf16[8,64,8]{1,0,2:T(8,128)(2,1)S(1)}, u32[]{:S(2)}, u32[]{:S(2)}) collective-permute-start(bf16[8,64,8]{1,0,2:T(8,128)(2,1)S(1)} %reshape.358), channel_id=1, source_target_pairs={{4,0},{8,4},{12,8},{16,12},{20,16},{24,20},{28,24},{0,28},{5,1},{9... | collective-permute-start | bytes 24584 | tf_op jit(solution)/shard_map/ppermute | solution.py:186
  209.9 6.4 %collective-permute-start.2 = (bf16[8,64,8]{1,0,2:T(8,128)(2,1)S(1)}, bf16[8,64,8]{1,0,2:T(8,128)(2,1)S(1)}, u32[]{:S(2)}, u32[]{:S(2)}) collective-permute-start(bf16[8,64,8]{1,0,2:T(8,128)(2,1)S(1)} %collective-permute-done.1), channel_id=1, source_target_pairs={{0,4},{4,8},{8,12},{12,16},{16,20},{20,24},{24,28},{28,0},{1,5},{5... | collective-permute-start | bytes 24584 | tf_op jit(solution)/shard_map/ppermute | solution.py:184
  210.1 6.9 %collective-permute-start.5 = (bf16[8,64,8]{1,0,2:T(8,128)(2,1)S(1)}, bf16[8,64,8]{1,0,2:T(8,128)(2,1)S(1)}, u32[]{:S(2)}, u32[]{:S(2)}) collective-permute-start(bf16[8,64,8]{1,0,2:T(8,128)(2,1)S(1)} %collective-permute-done.4), channel_id=1, source_target_pairs={{4,0},{8,4},{12,8},{16,12},{20,16},{24,20},{28,24},{0,28},{5,1},{9... | collective-permute-start | bytes 24584 | tf_op jit(solution)/shard_map/ppermute | solution.py:186
  216.4 6.4 %collective-permute-start.3 = (bf16[8,64,8]{1,0,2:T(8,128)(2,1)S(1)}, bf16[8,64,8]{1,0,2:T(8,128)(2,1)S(1)}, u32[]{:S(2)}, u32[]{:S(2)}) collective-permute-start(bf16[8,64,8]{1,0,2:T(8,128)(2,1)S(1)} %collective-permute-done.2), channel_id=1, source_target_pairs={{0,4},{4,8},{8,12},{12,16},{16,20},{20,24},{24,28},{28,0},{1,5},{5... | collective-permute-start | bytes 24584 | tf_op jit(solution)/shard_map/ppermute | solution.py:184
  217.0 6.2 %collective-permute-start.6 = (bf16[8,64,8]{1,0,2:T(8,128)(2,1)S(1)}, bf16[8,64,8]{1,0,2:T(8,128)(2,1)S(1)}, u32[]{:S(2)}, u32[]{:S(2)}) collective-permute-start(bf16[8,64,8]{1,0,2:T(8,128)(2,1)S(1)} %collective-permute-done.5), channel_id=1, source_target_pairs={{4,0},{8,4},{12,8},{16,12},{20,16},{24,20},{28,24},{0,28},{5,1},{9... | collective-permute-start | bytes 24584 | tf_op jit(solution)/shard_map/ppermute | solution.py:186
  364.7 72.7 %copy-start.2 = (bf16[4,32,4096]{2,1,0:T(8,128)(2,1)S(1)}, bf16[4,32,4096]{2,1,0:T(8,128)(2,1)}, u32[]{:S(2)}) copy-start(bf16[4,32,4096]{2,1,0:T(8,128)(2,1)} %param.19) | copy-start | bytes 3145732
  364.7 72.7 %copy-start.11 = (f32[32]{0:T(128)S(1)}, f32[32]{0:T(128)}, u32[]{:S(2)}) copy-start(f32[32]{0:T(128)} %param.33) | copy-start | bytes 388
  (6 other events, 53.2 us)
Sparse Core Ops, SparseCore 0:
  18.5 33.1 all-reduce.8
  136.5 31.6 all-reduce.6
  364.9 72.5 reduce-scatter.1
